TPU v7x, 512 devices: a whole 4x4x16 slice. The times are simulated.
512 devices in a mesh: grp: 16 (over z), shard: 32 (over y, x, core).
Axes of the slice: x: 4, y: 4, z: 16, core: 2. Of those that a mesh axis runs over, the one named last changes fastest.
Arguments:
- activations: bfloat16 [1024, 5120], P('grp', 'shard'), may hold values from -6 to 6
- grad_outputs: bfloat16 [1024, 27648], P('shard', 'grp'), may hold values from -6 to 6
- basis_in: bfloat16 [5120, 2560], P('shard', 'grp'), may hold values from -0.078125 to 0.078125
- basis_out: bfloat16 [27648, 13824], P('grp', 'shard'), may hold values from -0.0390625 to 0.0390625
- query_grads: bfloat16 [16, 2560, 13824], P('grp', None, 'shard'), may hold values from -0.0009765625 to 0.0009765625
Outputs:
- scores: float32 [16, 1024], P('grp', 'shard')
All inputs are finite; a program needn't handle non-finite values.
Results may differ from a plain program's by a relative error of at most 0.0041.
Values may be sent and summed in bfloat16 or wider, within the bound.
No kernel may reach another device: no remote copies, remote signals or barrier semaphores. Data moves between devices by JAX's collectives and lax.ppermute only.
A program may use at most 64 MiB of HBM per device.

v0:
```python
import jax
import jax.numpy as jnp
from jax import lax
from jax.sharding import PartitionSpec as P


def local(activations, grad_outputs, basis_in, basis_out, query_grads):
    full_in = lax.all_gather(basis_in, "grp", axis=1, tiled=True)
    act_terms = lax.dot_general(
        full_in, activations, (((0,), (1,)), ((), ())), preferred_element_type=jnp.float32
    )
    act_local = lax.psum(act_terms, "shard").astype(jnp.bfloat16)
    act_rot = lax.all_gather(act_local, "grp", axis=1, tiled=True)
    out_terms = jnp.dot(
        lax.all_gather(grad_outputs, "shard", axis=0, tiled=True),
        basis_out,
        preferred_element_type=jnp.float32,
    )
    out_rot = lax.psum(out_terms, "grp").astype(jnp.bfloat16)
    mixed = lax.dot_general(
        act_rot, query_grads[0], (((0,), (0,)), ((), ())), preferred_element_type=jnp.float32
    )
    partial_scores = jnp.sum(mixed * out_rot.astype(jnp.float32), axis=1)
    return lax.psum_scatter(partial_scores[None, :], "shard", scatter_dimension=1, tiled=True)


def solution(mesh):
    placed = (
        P("grp", "shard"),
        P("shard", "grp"),
        P("shard", "grp"),
        P("grp", "shard"),
        P("grp", None, "shard"),
    )
    return jax.shard_map(
        local, mesh=mesh, in_specs=placed, out_specs=P("grp", "shard"), check_vma=False
    )
```

profile of v0, /device:TPU:2, one launch (start us, length us, event | category | flops | bytes accessed | tf_op | source)
XLA Modules:
  0.0 392.9 jit_solution(17154068372020771227)
XLA Ops:
  6.5 0.0 copy-start
  6.5 0.0 all-gather.5.cloned.1.call-start
  6.5 0.7 all-gather.5.cloned.1.call-update
  7.3 0.0 all-gather.3.cloned.1.call-start
  7.3 1.0 copy.6
  8.3 43.3 %all_gather.9 = bf16[160,2560]{0,1:T(8,128)(2,1)S(1)} all-gather(bf16[160,160]{0,1:T(8,128)(2,1)S(1)} %copy.6), channel_id=1, replica_groups=mesh['grp'=16,'shard'=32] {'grp'}, dimensions={1}, use_global_device_ids=true | all-gather | bytes 870400 | tf_op jit(solution)/shard_map/all_gather | solution.py:8
  51.6 1.3 fusion.4
  52.9 126.1 %all-reduce.3 = bf16[2560,64]{0,1:T(8,128)(2,1)} all-reduce(f32[2560,64]{0,1:T(8,128)S(1)} %fusion.4), channel_id=1, replica_groups=mesh['grp'=16,'shard'=32] {'shard'}, use_global_device_ids=true, to_apply=%region_0.0 | all-reduce | flops 163840 | bytes 983040 | tf_op jit(solution)/shard_map/psum | solution.py:12
  178.9 0.0 all-gather.3.cloned.1.call-update
  179.0 0.0 reduce-scatter.4.cloned.1.call-start
  179.0 0.0 all-gather.5.cloned.1.call-done
  179.0 5.5 %fusion.5 = f32[1024,432]{0,1:T(8,128)} fusion(bf16[1024,1728]{1,0:T(8,128)(2,1)} %all-gather.5.cloned.1.call-done, bf16[1728,432]{0,1:T(8,128)(2,1)} %param.8), kind=kOutput, calls=%fused_computation.4 | convolution fusion | flops 1528823808 | bytes 6801408 | tf_op jit(solution)/shard_map/dot_general | solution.py:14
  184.6 91.9 %all-reduce.2 = bf16[1024,432]{0,1:T(8,128)(2,1)S(1)} all-reduce(f32[1024,432]{0,1:T(8,128)} %fusion.5), channel_id=1, replica_groups=mesh['grp'=16,'shard'=32] {'grp'}, use_global_device_ids=true, to_apply=%region_1.0 | all-reduce | flops 442368 | bytes 2654208 | tf_op jit(solution)/shard_map/psum | solution.py:19
  276.4 4.1 %all-gather.3.cloned.1.call-done = bf16[2560,1024]{0,1:T(8,128)(2,1)} async-done(((bf16[2560,64]{0,1:T(8,128)(2,1)}), bf16[2560,1024]{0,1:T(8,128)(2,1)}) %all-gather.3.cloned.1.call-update) | async-done | bytes 5242896 | tf_op jit(solution)/shard_map/all_gather | solution.py:13
  280.5 0.0 copy-done
  280.5 5.0 %multiply_reduce_fusion = f32[1024]{0:T(1024)S(1)} fusion(bf16[2560,1024]{0,1:T(8,128)(2,1)} %all-gather.3.cloned.1.call-done, bf16[1,2560,432]{1,2,0:T(8,128)(2,1)S(1)} %copy-done, bf16[1024,432]{0,1:T(8,128)(2,1)S(1)} %all-reduce.2), kind=kOutput, calls=%fused_computation.2 | convolution fusion | flops 2266250240 | bytes 8343552 | tf_op jit(solution)/shard_map/dot_general | solution.py:20
  285.5 1.0 copy.7
  286.5 0.0 reduce-scatter.4.cloned.1.call-update
  286.5 98.5 %reduce-scatter.4.cloned.1.call-done = f32[32,1]{1,0:T(8,128)} async-done(((f32[1024,1]{1,0:T(8,128)}), f32[32,1]{1,0:T(8,128)}) %reduce-scatter.4.cloned.1.call-update) | async-done | bytes 144
  385.1 1.3 copy.8
Async XLA Ops:
  6.5 274.0 %copy-start = (bf16[1,2560,432]{1,2,0:T(8,128)(2,1)S(1)}, bf16[1,2560,432]{1,2,0:T(8,128)(2,1)}, u32[]{:S(2)}) copy-start(bf16[1,2560,432]{1,2,0:T(8,128)(2,1)} %param.9) | copy-start | bytes 6635524
  6.5 172.5 %all-gather.5.cloned.1.call-start = ((), (), s32[]{:S(2)}) async-start(), calls=%async_computation.2 | async-start | bytes 3784704 | tf_op jit(solution)/shard_map/all_gather | solution.py:15
  7.3 273.3 %all-gather.3.cloned.1.call-start = ((), (), s32[]{:S(2)}) async-start(), calls=%async_computation.1 | async-start | bytes 5570560 | tf_op jit(solution)/shard_map/all_gather | solution.py:13
  179.0 206.1 %reduce-scatter.4.cloned.1.call-start = ((), (), s32[]{:S(2)}) async-start(), calls=%async_computation.3 | async-start | bytes 540672
Sparse Core Ops, SparseCore 0:
  10.5 64.9 all-gather.4
  179.1 101.3 all-gather.2
  286.7 98.3 reduce-scatter.3
where the time goes:
time: 393 us
  blocking collectives  261 us (66%)
  waiting for transfers between devices  103 us (26%)
  between operations  13.1 us (3%)
  matrix products  11.8 us (3%)
    psum x1, blocking collectives, local(): act_local = lax.psum(act_terms, 'shard').astype(jnp.bfloat16)  126 us
    unnamed x4, waiting for transfers between devices  99.3 us
    psum x1, blocking collectives, local(): out_rot = lax.psum(out_terms, 'grp').astype(jnp.bfloat16)  91.9 us
    all_gather x1, blocking collectives, local(): full_in = lax.all_gather(basis_in, 'grp', axis=1, tiled=True)  43.3 us
  transfers between devices with their start and end apart: 3, of which 2 were waited for; matrix products, arithmetic and copies ran while one was open for 2% of the time, Pallas kernels for 0%

commit v1 on v0

--- a/solution.py
+++ b/solution.py
@@ -5,7 +5,9 @@
 
 
 def local(activations, grad_outputs, basis_in, basis_out, query_grads):
-    full_in = lax.all_gather(basis_in, "grp", axis=1, tiled=True)
+    full_in = jnp.concatenate(
+        lax.all_to_all(jnp.stack([basis_in] * lax.axis_size("grp")), "grp", 0, 0), axis=1
+    )
     act_terms = lax.dot_general(
         full_in, activations, (((0,), (1,)), ((), ())), preferred_element_type=jnp.float32
     )

time: 393 us -> 435 us (1.11)
  blocking collectives: 261 us -> 301 us
    all_to_all x0 -> x1, blocking collectives: none -> 78.7 us  [local(): lax.all_to_all(jnp.stack([basis_in] * lax.axis_size('grp')), 'grp', 0, 0)]
    all_gather x1 -> x0, blocking collectives: 43.3 us -> none  [local(): full_in = lax.all_gather(basis_in, 'grp', axis=1, tiled=True)]
    psum x1, blocking collectives: 91.9 us -> 97.2 us  [local(): out_rot = lax.psum(out_terms, 'grp').astype(jnp.bfloat16)]
  transfers between devices with their start and end apart: 3 -> 3, of which waited for: 2 -> 2; matrix products, arithmetic and copies ran while one was open for 2% -> 3% of each run, Pallas kernels for 0% -> 0%
where the time goes in v1:
time: 435 us
  blocking collectives  301 us (69%)
  waiting for transfers between devices  102 us (23%)
  between operations  13.2 us (3%)
  matrix products  11.9 us (3%)
  local copies, waits for them, and re-layouts  6.79 us (2%)
    psum x1, blocking collectives, local(): act_local = lax.psum(act_terms, 'shard').astype(jnp.bfloat16)  125 us
    unnamed x4, waiting for transfers between devices  99.5 us
    psum x1, blocking collectives, local(): out_rot = lax.psum(out_terms, 'grp').astype(jnp.bfloat16)  97.2 us
    all_to_all x1, blocking collectives, local(): lax.all_to_all(jnp.stack([basis_in] * lax.axis_size('grp')), 'grp', 0, 0)  78.7 us
  transfers between devices with their start and end apart: 3, of which 2 were waited for; matrix products, arithmetic and copies ran while one was open for 3% of the time, Pallas kernels for 0%

profile of v1, /device:TPU:2, one launch (start us, length us, event | category | flops | bytes accessed | tf_op | source)
XLA Modules:
  0.0 435.0 jit_solution(5549883376780402374)
XLA Ops:
  6.5 0.0 copy-start
  6.5 0.0 all-gather.5.cloned.1.call-start
  6.5 0.7 all-gather.5.cloned.1.call-update
  7.3 0.0 all-gather.3.cloned.1.call-start
  7.3 1.0 stack.2
  8.3 78.7 %all_to_all.5 = bf16[16,160,160]{2,1,0:T(8,128)(2,1)S(1)} all-to-all(bf16[16,160,160]{2,1,0:T(8,128)(2,1)S(1)} %stack.2), channel_id=1, replica_groups=mesh['grp'=16,'shard'=32] {'grp'}, dimensions={0} | all-to-all | bytes 1638400 | tf_op jit(solution)/shard_map/all_to_all | solution.py:9
  87.0 0.0 copy-start.1
  87.0 0.7 copy.6
  87.7 2.7 reshape.9
  90.5 0.0 copy-done.1
  90.5 1.4 fusion.5
  91.9 125.2 %all-reduce.3 = bf16[2560,64]{0,1:T(8,128)(2,1)} all-reduce(f32[2560,64]{0,1:T(8,128)S(1)} %fusion.5), channel_id=1, replica_groups=mesh['grp'=16,'shard'=32] {'shard'}, use_global_device_ids=true, to_apply=%region_0.0 | all-reduce | flops 163840 | bytes 983040 | tf_op jit(solution)/shard_map/psum | solution.py:14
  217.1 0.0 all-gather.3.cloned.1.call-update
  217.1 0.0 reduce-scatter.4.cloned.1.call-start
  217.2 0.0 all-gather.5.cloned.1.call-done
  217.2 5.5 %fusion.4 = f32[1024,432]{0,1:T(8,128)} fusion(bf16[1024,1728]{1,0:T(8,128)(2,1)} %all-gather.5.cloned.1.call-done, bf16[1728,432]{0,1:T(8,128)(2,1)} %param.8), kind=kOutput, calls=%fused_computation.3 | convolution fusion | flops 1528823808 | bytes 6801408 | tf_op jit(solution)/shard_map/dot_general | solution.py:16
  222.7 97.2 %all-reduce.2 = bf16[1024,432]{0,1:T(8,128)(2,1)S(1)} all-reduce(f32[1024,432]{0,1:T(8,128)} %fusion.4), channel_id=1, replica_groups=mesh['grp'=16,'shard'=32] {'grp'}, use_global_device_ids=true, to_apply=%region_1.0 | all-reduce | flops 442368 | bytes 2654208 | tf_op jit(solution)/shard_map/psum | solution.py:21
  320.0 2.5 all-gather.3.cloned.1.call-done
  322.4 0.0 copy-done
  322.4 5.0 %multiply_reduce_fusion = f32[1024]{0:T(1024)S(1)} fusion(bf16[2560,1024]{0,1:T(8,128)(2,1)} %all-gather.3.cloned.1.call-done, bf16[1,2560,432]{1,2,0:T(8,128)(2,1)S(1)} %copy-done, bf16[1024,432]{0,1:T(8,128)(2,1)S(1)} %all-reduce.2), kind=kOutput, calls=%fused_computation.2 | convolution fusion | flops 2266250240 | bytes 8343552 | tf_op jit(solution)/shard_map/dot_general | solution.py:22
  327.4 1.0 copy.7
  328.4 0.0 reduce-scatter.4.cloned.1.call-update
  328.5 98.7 %reduce-scatter.4.cloned.1.call-done = f32[32,1]{1,0:T(8,128)} async-done(((f32[1024,1]{1,0:T(8,128)}), f32[32,1]{1,0:T(8,128)}) %reduce-scatter.4.cloned.1.call-update) | async-done | bytes 144
  427.2 1.3 copy.8
Async XLA Ops:
  6.5 315.9 %copy-start = (bf16[1,2560,432]{1,2,0:T(8,128)(2,1)S(1)}, bf16[1,2560,432]{1,2,0:T(8,128)(2,1)}, u32[]{:S(2)}) copy-start(bf16[1,2560,432]{1,2,0:T(8,128)(2,1)} %param.9) | copy-start | bytes 6635524
  6.5 210.7 %all-gather.5.cloned.1.call-start = ((), (), s32[]{:S(2)}) async-start(), calls=%async_computation.3 | async-start | bytes 3784704 | tf_op jit(solution)/shard_map/all_gather | solution.py:17
  7.3 315.2 %all-gather.3.cloned.1.call-start = ((), (), s32[]{:S(2)}) async-start(), calls=%async_computation.2 | async-start | bytes 5570560 | tf_op jit(solution)/shard_map/all_gather | solution.py:15
  87.0 3.5 copy-start.1
  217.1 210.1 %reduce-scatter.4.cloned.1.call-start = ((), (), s32[]{:S(2)}) async-start(), calls=%async_computation.4 | async-start | bytes 540672
Sparse Core Ops, SparseCore 0:
  10.5 64.9 all-gather.4
  217.2 105.1 all-gather.2
  328.6 98.5 reduce-scatter.3

commit v2 on v0

--- a/solution.py
+++ b/solution.py
@@ -16,7 +16,7 @@
         basis_out,
         preferred_element_type=jnp.float32,
     )
-    out_rot = lax.psum(out_terms, "grp").astype(jnp.bfloat16)
+    out_rot = jnp.sum(lax.all_gather(out_terms, "grp"), axis=0).astype(jnp.bfloat16)
     mixed = lax.dot_general(
         act_rot, query_grads[0], (((0,), (0,)), ((), ())), preferred_element_type=jnp.float32
     )

time: 393 us -> 584 us (1.49)
  waiting for transfers between devices: 103 us -> 352 us
  blocking collectives: 261 us -> 174 us
  local copies, waits for them, and re-layouts: 3.31 us -> 28.9 us
    all_gather x0 -> x1, waiting for transfers between devices: none -> 139 us  [local(): lax.all_gather(out_terms, 'grp')]
    psum x1 -> x0, blocking collectives: 91.9 us -> none  [local(): out_rot = lax.psum(out_terms, 'grp').astype(jnp.bfloat16)]
    all_gather x1, waiting for transfers between devices: 0.02 us -> 68.1 us  [local(): lax.all_gather(grad_outputs, 'shard', axis=0, tiled=True)]
    all_gather x1, waiting for transfers between devices: 4.07 us -> 47.2 us  [local(): act_rot = lax.all_gather(act_local, 'grp', axis=1, tiled=True)]
    unnamed x5 -> x10, local copies, waits for them, and re-layouts: 3.31 us -> 28.9 us
    unnamed x4 -> x5, waiting for transfers between devices: 99.3 us -> 97.3 us
  transfers between devices with their start and end apart: 3 -> 4, of which waited for: 2 -> 4; matrix products, arithmetic and copies ran while one was open for 2% -> 6% of each run, Pallas kernels for 0% -> 0%
where the time goes in v2:
time: 584 us
  waiting for transfers between devices  352 us (60%)
  blocking collectives  174 us (30%)
  local copies, waits for them, and re-layouts  28.9 us (5%)
  between operations  13.2 us (2%)
  matrix products  11 us (2%)
    all_gather x1, waiting for transfers between devices, local(): lax.all_gather(out_terms, 'grp')  139 us
    psum x1, blocking collectives, local(): act_local = lax.psum(act_terms, 'shard').astype(jnp.bfloat16)  125 us
    unnamed x5, waiting for transfers between devices  97.3 us
    all_gather x1, waiting for transfers between devices, local(): lax.all_gather(grad_outputs, 'shard', axis=0, tiled=True)  68.1 us
    all_gather x1, blocking collectives, local(): full_in = lax.all_gather(basis_in, 'grp', axis=1, tiled=True)  48.6 us
    all_gather x1, waiting for transfers between devices, local(): act_rot = lax.all_gather(act_local, 'grp', axis=1, tiled=True)  47.2 us
    unnamed x10, local copies, waits for them, and re-layouts  28.9 us
  transfers between devices with their start and end apart: 4, of which 4 were waited for; matrix products, arithmetic and copies ran while one was open for 6% of the time, Pallas kernels for 0%

profile of v2, /device:TPU:2, one launch (start us, length us, event | category | flops | bytes accessed | tf_op | source)
XLA Modules:
  0.0 584.2 jit_solution(3614422358583993850)
XLA Ops:
  6.5 0.0 copy-start
  6.5 0.0 all-gather.7.cloned.1.call-start
  6.5 0.7 all-gather.7.cloned.1.call-update
  7.3 0.0 copy-start.1
  7.3 0.0 all-gather.9.cloned.1.call-start
  7.3 68.1 %all-gather.7.cloned.1.call-done = bf16[1024,1728]{1,0:T(8,128)(2,1)} async-done(((bf16[32,1728]{1,0:T(8,128)(2,1)}), bf16[1024,1728]{1,0:T(8,128)(2,1)}) %all-gather.7.cloned.1.call-update) | async-done | bytes 3538960 | tf_op jit(solution)/shard_map/all_gather | solution.py:15
  75.5 5.5 fusion.5
  81.0 0.0 copy-start.2
  81.0 0.0 all-gather.9.cloned.1.call-update
  81.0 0.0 all-gather.5.cloned.1.call-start
  81.0 0.0 copy-done.1
  81.0 0.1 copy.6
  81.1 48.6 %all_gather.15 = bf16[160,2560]{0,1:T(8,128)(2,1)S(1)} all-gather(bf16[160,160]{0,1:T(8,128)(2,1)S(1)} %copy.6), channel_id=1, replica_groups=mesh['grp'=16,'shard'=32] {'grp'}, dimensions={1}, use_global_device_ids=true | all-gather | bytes 870400 | tf_op jit(solution)/shard_map/all_gather | solution.py:8
  129.7 0.0 copy-done.2
  129.7 0.5 fusion.4
  130.2 125.4 %all-reduce.1 = bf16[2560,64]{0,1:T(8,128)(2,1)} all-reduce(f32[2560,64]{0,1:T(8,128)S(1)} %fusion.4), channel_id=1, replica_groups=mesh['grp'=16,'shard'=32] {'shard'}, use_global_device_ids=true, to_apply=%region_0.0 | all-reduce | flops 163840 | bytes 983040 | tf_op jit(solution)/shard_map/psum | solution.py:12
  255.7 0.0 all-gather.5.cloned.1.call-update
  255.7 0.0 reduce-scatter.4.cloned.1.call-start
  255.7 138.9 %all-gather.9.cloned.1.call-done = f32[16384,432]{0,1:T(8,128)} async-done(((f32[1024,432]{0,1:T(8,128)}), f32[16384,432]{0,1:T(8,128)}) %all-gather.9.cloned.1.call-update) | async-done | bytes 28311568 | tf_op jit(solution)/shard_map/all_gather | solution.py:19
  394.7 26.4 %copy.9 = f32[54,8,16,1024]{3,2,1,0:T(8,128)S(1)} copy(f32[54,8,16,1024]{3,1,2,0:T(8,128)} %bitcast.18) | data formatting | bytes 56623104
  421.1 5.4 bitcast_reduce_fusion
  426.5 47.2 %all-gather.5.cloned.1.call-done = bf16[2560,1024]{0,1:T(8,128)(2,1)} async-done(((bf16[2560,64]{0,1:T(8,128)(2,1)}), bf16[2560,1024]{0,1:T(8,128)(2,1)}) %all-gather.5.cloned.1.call-update) | async-done | bytes 5242896 | tf_op jit(solution)/shard_map/all_gather | solution.py:13
  473.8 0.0 copy-done
  473.8 5.0 multiply_reduce_fusion
  478.7 1.0 copy.7
  479.8 0.0 reduce-scatter.4.cloned.1.call-update
  479.8 96.6 %reduce-scatter.4.cloned.1.call-done = f32[32,1]{1,0:T(8,128)} async-done(((f32[1024,1]{1,0:T(8,128)}), f32[32,1]{1,0:T(8,128)}) %reduce-scatter.4.cloned.1.call-update) | async-done | bytes 144
  576.4 1.3 copy.8
Async XLA Ops:
  6.5 467.2 %copy-start = (bf16[1,2560,432]{1,2,0:T(8,128)(2,1)S(1)}, bf16[1,2560,432]{1,2,0:T(8,128)(2,1)}, u32[]{:S(2)}) copy-start(bf16[1,2560,432]{1,2,0:T(8,128)(2,1)} %param.9) | copy-start | bytes 6635524
  6.5 68.9 %all-gather.7.cloned.1.call-start = ((), (), s32[]{:S(2)}) async-start(), calls=%async_computation.2 | async-start | bytes 3784704 | tf_op jit(solution)/shard_map/all_gather | solution.py:15
  7.3 73.8 %copy-start.1 = (bf16[160,160]{1,0:T(8,128)(2,1)S(1)}, bf16[160,160]{1,0:T(8,128)(2,1)}, u32[]{:S(2)}) copy-start(bf16[160,160]{1,0:T(8,128)(2,1)} %param.7) | copy-start | bytes 153604
  7.3 387.4 %all-gather.9.cloned.1.call-start = ((), (), s32[]{:S(2)}) async-start(), calls=%async_computation.3 | async-start | bytes 30081024 | tf_op jit(solution)/shard_map/all_gather | solution.py:19
  81.0 48.8 %copy-start.2 = (bf16[64,160]{1,0:T(8,128)(2,1)S(1)}, bf16[64,160]{1,0:T(8,128)(2,1)}, u32[]{:S(2)}) copy-start(bf16[64,160]{1,0:T(8,128)(2,1)} %param.5) | copy-start | bytes 61444
  81.0 392.8 %all-gather.5.cloned.1.call-start = ((), (), s32[]{:S(2)}) async-start(), calls=%async_computation.1 | async-start | bytes 5570560 | tf_op jit(solution)/shard_map/all_gather | solution.py:13
  255.7 320.7 %reduce-scatter.4.cloned.1.call-start = ((), (), s32[]{:S(2)}) async-start(), calls=%async_computation.4 | async-start | bytes 540672
Sparse Core Ops, SparseCore 0:
  10.5 64.9 all-gather.6
  81.1 313.5 all-gather.8
  396.8 76.9 all-gather.4
  479.9 96.4 reduce-scatter.3
